TPU v7x, 128 devices: a whole 4x4x4 slice. The times are simulated.
128 devices in a mesh: elec: 8 (over y_lo, z), cell: 16 (over y_hi, x, core).
Axes of the slice: x: 4, y: 4 (y_hi: 2, y_lo: 2; y = y_hi * 2 + y_lo), z: 4, core: 2. Of those that a mesh axis runs over, the one named last changes fastest.
Arguments:
- grads: bfloat16 [3, 1024, 2048], P(None, 'elec', 'cell'), may hold values from -6 to 6
- quads: int32 [32768, 4], P('elec'), may hold values from 0 to 1023, all different within a row
- volume: float32 [2048], P('cell'), may hold values from 0.5 to 2
- weight: float32 [32768], P('elec'), may hold values from 0.5 to 2
Outputs:
- hessian: float32 [2048, 2048], P('elec', 'cell')
Inputs may be any that keep to these rules, and one draw needn't show every extreme that they name: `quads`: each row names four different electrodes; every electrode appears in some row.
All inputs are finite; a program needn't handle non-finite values.
Results may differ from a plain program's by a relative error of at most 0.00096.
Values may be sent and summed in bfloat16 or wider, within the bound.
A program may use at most 64 MiB of HBM per device.

v0:
```python
import jax
import jax.numpy as jnp
from jax import lax
from jax.sharding import PartitionSpec as P


def inner_rows(left, right):
    return lax.dot_general(
        left, right, (((0,), (0,)), ((), ())), preferred_element_type=jnp.float32
    )


def per_device(grads, quads, volume, weight):
    measured_rows = quads.shape[0]
    piece = lax.all_gather(grads, "elec", axis=1, tiled=True)
    width = piece.shape[1]
    labels = lax.iota(jnp.int32, width)
    source_map = (
        (quads[:, 0:1] == labels).astype(jnp.float32)
        - (quads[:, 1:2] == labels).astype(jnp.float32)
    ).astype(jnp.bfloat16)
    receive_map = (
        (quads[:, 2:3] == labels).astype(jnp.float32)
        - (quads[:, 3:4] == labels).astype(jnp.float32)
    ).astype(jnp.bfloat16)
    source = jnp.einsum("me,kec->kmc", source_map, piece, preferred_element_type=jnp.float32)
    receiver = jnp.einsum("me,kec->kmc", receive_map, piece, preferred_element_type=jnp.float32)
    source, receiver = (source, receiver)
    dots = source[0] * receiver[0] + source[1] * receiver[1] + source[2] * receiver[2]
    scaled_rows = (weight[:, None] * -(volume[None, :] * dots)).astype(jnp.bfloat16)
    term = inner_rows(lax.all_gather(scaled_rows, "cell", axis=1, tiled=True), scaled_rows)
    summed_rows = lax.psum_scatter(term, "elec", scatter_dimension=0, tiled=True)
    return summed_rows / jnp.float32(measured_rows * lax.axis_size("elec"))


def solution(mesh):
    placed = (P(None, "elec", "cell"), P("elec", None), P("cell"), P("elec"))
    return jax.shard_map(
        per_device, mesh=mesh, in_specs=placed, out_specs=P("elec", "cell"), check_vma=False
    )
```

profile of v0, /device:TPU:0, one launch (start us, length us, event | category | flops | bytes accessed | tf_op | source)
XLA Modules:
  0.0 235.7 jit_solution(18083217160854926386)
XLA Ops:
  6.5 0.0 all-gather.2.cloned.1.call-start
  6.5 1.1 fusion.23
  7.6 31.4 %all_gather.6 = bf16[3,1024,128]{2,1,0:T(8,128)(2,1)S(1)} all-gather(bf16[3,128,128]{2,1,0:T(8,128)(2,1)} %param.4), channel_id=1, replica_groups=mesh['elec'=8,'cell'=16] {'elec'}, dimensions={1}, use_global_device_ids=true | all-gather | bytes 884736 | tf_op jit(solution)/shard_map/all_gather | solution.py:15
  39.0 6.9 %fusion.10 = f32[3,4096,128]{2,1,0:T(8,128)S(1)} fusion(bf16[3,1024,128]{2,1,0:T(8,128)(2,1)S(1)} %all_gather.6, s32[4096]{0:T(1024)S(1)} %bitcast.34, s32[4096]{0:T(1024)S(1)} %bitcast.35), kind=kOutput, calls=%fused_computation.14 | convolution fusion | flops 3246391296 | bytes 7110656 | tf_op jit(solution)/shard_map/me,kec->kmc/dot_general | solution.py:27
  45.9 0.0 copy-start
  45.9 0.0 copy-start.1
  45.9 6.9 %fusion.13 = f32[3,4096,128]{2,1,0:T(8,128)S(1)} fusion(bf16[3,1024,128]{2,1,0:T(8,128)(2,1)S(1)} %all_gather.6, s32[4096]{0:T(1024)S(1)} %bitcast.33, s32[4096]{0:T(1024)S(1)} %bitcast.32), kind=kOutput, calls=%fused_computation.15 | convolution fusion | flops 3246391296 | bytes 7110656 | tf_op jit(solution)/shard_map/me,kec->kmc/dot_general | solution.py:26
  52.8 0.0 copy-done
  52.9 0.0 copy-done.1
  52.9 1.5 fusion.21
  54.4 0.0 all-gather.2.cloned.1.call-update
  54.4 0.0 reduce-scatter.2.cloned.1.call-start
  54.5 123.3 %all-gather.2.cloned.1.call-done = bf16[4096,2048]{1,0:T(8,128)(2,1)} async-done(((bf16[4096,128]{1,0:T(8,128)(2,1)}), bf16[4096,2048]{1,0:T(8,128)(2,1)}) %all-gather.2.cloned.1.call-update) | async-done | bytes 16777232 | tf_op jit(solution)/shard_map/all_gather | solution.py:31
  177.8 11.6 %fusion.24 = f32[2048,128]{1,0:T(8,128)} fusion(bf16[4096,2048]{1,0:T(8,128)(2,1)} %all-gather.2.cloned.1.call-done, bf16[4096,128]{1,0:T(8,128)(2,1)} %fusion.21), kind=kOutput, calls=%fused_computation.28 | convolution fusion | flops 2147483648 | bytes 18874368 | tf_op jit(solution)/shard_map/dot_general | solution.py:8
  189.4 0.0 reduce-scatter.2.cloned.1.call-update
  189.4 37.9 %reduce-scatter.2.cloned.1.call-done = f32[256,128]{1,0:T(8,128)} async-done(((f32[2048,128]{1,0:T(8,128)}), f32[256,128]{1,0:T(8,128)}) %reduce-scatter.2.cloned.1.call-update) | async-done | bytes 131088 | tf_op jit(solution)/shard_map/reduce_scatter | solution.py:32
  227.3 1.6 broadcast_multiply_fusion
Async XLA Ops:
  6.5 171.2 %all-gather.2.cloned.1.call-start = ((), (), s32[]{:S(2)}) async-start(), calls=%async_computation.1 | async-start | bytes 17825792 | tf_op jit(solution)/shard_map/all_gather | solution.py:31
  45.9 7.0 %copy-start = (f32[4096]{0:T(1024)S(1)}, f32[4096]{0:T(1024)}, u32[]{:S(2)}) copy-start(f32[4096]{0:T(1024)} %param.7) | copy-start | bytes 49156
  45.9 7.0 %copy-start.1 = (f32[128]{0:T(128)S(1)}, f32[128]{0:T(128)}, u32[]{:S(2)}) copy-start(f32[128]{0:T(128)} %param.6) | copy-start | bytes 1540
  54.4 172.9 %reduce-scatter.2.cloned.1.call-start = ((), (), s32[]{:S(2)}) async-start(), calls=%async_computation.2 | async-start | bytes 1179648 | tf_op jit(solution)/shard_map/reduce_scatter | solution.py:32
Sparse Core Ops, SparseCore 0:
  54.5 123.1 all-gather.1
  189.5 37.7 reduce-scatter.1
where the time goes:
time: 236 us
  waiting for transfers between devices  161 us (68%)
  blocking collectives  31.4 us (13%)
  matrix products  25.4 us (11%)
  between operations  13.5 us (6%)
  other arithmetic  3.1 us (1%)
    all_gather x1, waiting for transfers between devices, per_device(): lax.all_gather(scaled_rows, 'cell', axis=1, tiled=True)  123 us
    reduce_scatter x1, waiting for transfers between devices, per_device(): lax.psum_scatter(term, 'elec', scatter_dimension=0, tiled=True)  37.9 us
    all_gather x1, blocking collectives, per_device(): piece = lax.all_gather(grads, 'elec', axis=1, tiled=True)  31.4 us
    dot_general x1, matrix products, inner_rows(): lax.dot_general(left, right, (((0,), (0,)), ((), ())), preferred_element_...  11.6 us
    dot_general x1, matrix products, per_device(): jnp.einsum('me,kec->kmc', source_map, piece, preferred_element_type=jnp.f...  6.94 us
    dot_general x1, matrix products, per_device(): jnp.einsum('me,kec->kmc', receive_map, piece, preferred_element_type=jnp....  6.91 us
  transfers between devices with their start and end apart: 2, of which 2 were waited for; matrix products, arithmetic and copies ran while one was open for 0% of the time, Pallas kernels for 0%

commit v1 on v0

--- a/solution.py
+++ b/solution.py
@@ -12,7 +12,9 @@
 
 def per_device(grads, quads, volume, weight):
     measured_rows = quads.shape[0]
-    piece = lax.all_gather(grads, "elec", axis=1, tiled=True)
+    piece = jnp.concatenate(
+        lax.all_to_all(jnp.stack([grads] * lax.axis_size("elec")), "elec", 0, 0), axis=1
+    )
     width = piece.shape[1]
     labels = lax.iota(jnp.int32, width)
     source_map = (

time: 236 us -> 223 us (0.945)
  blocking collectives: 31.4 us -> 0 us
  waiting for transfers between devices: 161 us -> 171 us
  starting transfers between devices: 0.04 us -> 6.52 us
    all_gather x1 -> x0, blocking collectives: 31.4 us -> none  [per_device(): piece = lax.all_gather(grads, 'elec', axis=1, tiled=True)]
    all_to_all x0 -> x1, waiting for transfers between devices: none -> 10.9 us  [per_device(): lax.all_to_all(jnp.stack([grads] * lax.axis_size('elec')), 'elec', 0, 0)]
    all_to_all x0 -> x1, starting transfers between devices: none -> 6.44 us  [per_device(): lax.all_to_all(jnp.stack([grads] * lax.axis_size('elec')), 'elec', 0, 0)]
  transfers between devices with their start and end apart: 2 -> 3, of which waited for: 2 -> 3; matrix products, arithmetic and copies ran while one was open for 0% -> 0% of each run, Pallas kernels for 0% -> 0%
where the time goes in v1:
time: 223 us
  waiting for transfers between devices  171 us (77%)
  matrix products  25.6 us (11%)
  between operations  13.5 us (6%)
  starting transfers between devices  6.52 us (3%)
  other arithmetic  3.09 us (1%)
  local copies, waits for them, and re-layouts  3.08 us (1%)
    all_gather x1, waiting for transfers between devices, per_device(): lax.all_gather(scaled_rows, 'cell', axis=1, tiled=True)  122 us
    reduce_scatter x1, waiting for transfers between devices, per_device(): lax.psum_scatter(term, 'elec', scatter_dimension=0, tiled=True)  37.9 us
    dot_general x1, matrix products, inner_rows(): lax.dot_general(left, right, (((0,), (0,)), ((), ())), preferred_element_...  11.6 us
    all_to_all x1, waiting for transfers between devices, per_device(): lax.all_to_all(jnp.stack([grads] * lax.axis_size('elec')), 'elec', 0, 0)  10.9 us
    dot_general x1, matrix products, per_device(): jnp.einsum('me,kec->kmc', receive_map, piece, preferred_element_type=jnp....  7 us
    dot_general x1, matrix products, per_device(): jnp.einsum('me,kec->kmc', source_map, piece, preferred_element_type=jnp.f...  6.98 us
    all_to_all x1, starting transfers between devices, per_device(): lax.all_to_all(jnp.stack([grads] * lax.axis_size('elec')), 'elec', 0, 0)  6.44 us
  transfers between devices with their start and end apart: 3, of which 3 were waited for; matrix products, arithmetic and copies ran while one was open for 0% of the time, Pallas kernels for 0%

profile of v1, /device:TPU:0, one launch (start us, length us, event | category | flops | bytes accessed | tf_op | source)
XLA Modules:
  0.0 222.6 jit_solution(7136416878336491439)
XLA Ops:
  6.5 2.0 stack.2
  8.5 6.4 %all-to-all-start = ((bf16[8,3,128,128]{3,2,1,0:T(8,128)(2,1)}), bf16[8,3,128,128]{3,2,1,0:T(8,128)(2,1)S(1)}, u32[]{:S(2)}, u32[]{:S(2)}) async-start(bf16[8,3,128,128]{3,2,1,0:T(8,128)(2,1)} %stack.2), calls=%async_computation | async-start | bytes 1572864 | tf_op jit(solution)/shard_map/all_to_all | solution.py:16
  14.9 0.0 all-gather.2.cloned.1.call-start
  15.0 1.1 fusion.23
  16.0 10.9 %all-to-all-done = bf16[8,3,128,128]{3,2,1,0:T(8,128)(2,1)S(1)} async-done(((bf16[8,3,128,128]{3,2,1,0:T(8,128)(2,1)}), bf16[8,3,128,128]{3,2,1,0:T(8,128)(2,1)S(1)}, u32[]{:S(2)}, u32[]{:S(2)}) %all-to-all-start) | async-done | bytes 786464 | tf_op jit(solution)/shard_map/all_to_all | solution.py:16
  26.9 0.1 copy.5
  27.0 7.0 %fusion.10 = f32[3,4096,128]{2,1,0:T(8,128)S(1)} fusion(bf16[3,1024,128]{2,1,0:T(8,128)(2,1)S(1)} %bitcast.35, s32[4096]{0:T(1024)S(1)} %bitcast.39, s32[4096]{0:T(1024)S(1)} %bitcast.40), kind=kOutput, calls=%fused_computation.14 | convolution fusion | flops 3246391296 | bytes 7110656 | tf_op jit(solution)/shard_map/me,kec->kmc/dot_general | solution.py:29
  34.0 0.0 copy-start
  34.0 0.0 copy-start.1
  34.0 7.0 %fusion.13 = f32[3,4096,128]{2,1,0:T(8,128)S(1)} fusion(bf16[3,1024,128]{2,1,0:T(8,128)(2,1)S(1)} %bitcast.36, s32[4096]{0:T(1024)S(1)} %bitcast.38, s32[4096]{0:T(1024)S(1)} %bitcast.37), kind=kOutput, calls=%fused_computation.15 | convolution fusion | flops 3246391296 | bytes 7110656 | tf_op jit(solution)/shard_map/me,kec->kmc/dot_general | solution.py:28
  41.0 0.0 copy-done
  41.0 0.0 copy-done.1
  41.0 1.5 fusion.21
  42.5 0.0 all-gather.2.cloned.1.call-update
  42.6 0.0 reduce-scatter.2.cloned.1.call-start
  42.6 122.1 %all-gather.2.cloned.1.call-done = bf16[4096,2048]{1,0:T(8,128)(2,1)} async-done(((bf16[4096,128]{1,0:T(8,128)(2,1)}), bf16[4096,2048]{1,0:T(8,128)(2,1)}) %all-gather.2.cloned.1.call-update) | async-done | bytes 16777232 | tf_op jit(solution)/shard_map/all_gather | solution.py:33
  164.7 11.6 %fusion.24 = f32[2048,128]{1,0:T(8,128)} fusion(bf16[4096,2048]{1,0:T(8,128)(2,1)} %all-gather.2.cloned.1.call-done, bf16[4096,128]{1,0:T(8,128)(2,1)} %fusion.21), kind=kOutput, calls=%fused_computation.28 | convolution fusion | flops 2147483648 | bytes 18874368 | tf_op jit(solution)/shard_map/dot_general | solution.py:8
  176.3 0.0 reduce-scatter.2.cloned.1.call-update
  176.3 37.9 %reduce-scatter.2.cloned.1.call-done = f32[256,128]{1,0:T(8,128)} async-done(((f32[2048,128]{1,0:T(8,128)}), f32[256,128]{1,0:T(8,128)}) %reduce-scatter.2.cloned.1.call-update) | async-done | bytes 131088 | tf_op jit(solution)/shard_map/reduce_scatter | solution.py:34
  214.2 1.6 broadcast_multiply_fusion
Async XLA Ops:
  8.5 18.4 %all-to-all-start = ((bf16[8,3,128,128]{3,2,1,0:T(8,128)(2,1)}), bf16[8,3,128,128]{3,2,1,0:T(8,128)(2,1)S(1)}, u32[]{:S(2)}, u32[]{:S(2)}) async-start(bf16[8,3,128,128]{3,2,1,0:T(8,128)(2,1)} %stack.2), calls=%async_computation | async-start | bytes 1572864 | tf_op jit(solution)/shard_map/all_to_all | solution.py:16
  14.9 149.8 %all-gather.2.cloned.1.call-start = ((), (), s32[]{:S(2)}) async-start(), calls=%async_computation.2 | async-start | bytes 17825792 | tf_op jit(solution)/shard_map/all_gather | solution.py:33
  34.0 7.0 %copy-start = (f32[4096]{0:T(1024)S(1)}, f32[4096]{0:T(1024)}, u32[]{:S(2)}) copy-start(f32[4096]{0:T(1024)} %param.7) | copy-start | bytes 49156
  34.0 7.0 %copy-start.1 = (f32[128]{0:T(128)S(1)}, f32[128]{0:T(128)}, u32[]{:S(2)}) copy-start(f32[128]{0:T(128)} %param.6) | copy-start | bytes 1540
  42.6 171.6 %reduce-scatter.2.cloned.1.call-start = ((), (), s32[]{:S(2)}) async-start(), calls=%async_computation.3 | async-start | bytes 1179648 | tf_op jit(solution)/shard_map/reduce_scatter | solution.py:34
Sparse Core Ops, SparseCore 0:
  42.7 121.9 all-gather.1
  176.4 37.7 reduce-scatter.1
